TPU v7x, 128 devices: a whole 4x4x4 slice. The times are simulated.
128 devices in a mesh: tm: 4 (over z_hi, core), mic: 32 (over y, x, z_lo).
Axes of the slice: x: 4, y: 4, z: 4 (z_hi: 2, z_lo: 2; z = z_hi * 2 + z_lo), core: 2. Of those that a mesh axis runs over, the one named last changes fastest.
Arguments:
- samples: bfloat16 [32, 4096, 4096], P('tm', 'mic'), may hold values from -6 to 6
- bin_ids: int32 [16], replicated, may hold values from 1 to 2047
- delays: int32 [4096, 4096], P('mic'), may hold values from 0 to 1023
Outputs:
- source_map: float32 [16, 4096], P('tm', 'mic')
All inputs are finite; a program needn't handle non-finite values.
Results may differ from a plain program's by a relative error of at most 0.0013.
Values may be sent and summed in bfloat16 or wider, within the bound.
No kernel may reach another device: no remote copies, remote signals or barrier semaphores. Data moves between devices by JAX's collectives and lax.ppermute only.
A program may use at most 64 MiB of HBM per device.

v0:
```python
import math
import jax
import jax.numpy as jnp
from jax import lax
from jax.sharding import PartitionSpec as P


def dft_table(bin_ids, length):
    sample_index = jnp.arange(length, dtype=jnp.int32)
    window = 0.5 - 0.5 * jnp.cos(2.0 * jnp.pi * sample_index.astype(jnp.float32) / length)
    window_norm = jnp.sqrt(jnp.sum(window * window))
    phase_index = sample_index[:, None] * bin_ids[None, :] % length
    angles = 2.0 * jnp.pi * phase_index.astype(jnp.float32) / length
    cosine = window[:, None] * jnp.cos(angles) / window_norm
    sine_part = -window[:, None] * jnp.sin(angles) / window_norm
    return jnp.stack([cosine, sine_part], axis=-1).reshape(length, -1).astype(jnp.bfloat16)


def steer_block(received, delay_cols, bins_owned, length):
    seg_count = received.shape[0]
    mic_count = received.shape[3]
    point_count = delay_cols.shape[0]

    def per_bin(entry):
        bin_value, values = entry
        phases = 2.0 * jnp.pi * (bin_value * delay_cols % length).astype(jnp.float32) / length
        steer_rows = jnp.concatenate([jnp.cos(phases), jnp.sin(phases)], axis=0).astype(
            jnp.bfloat16
        )
        product = lax.dot_general(
            values.reshape(seg_count * 2, mic_count),
            steer_rows,
            (((1,), (1,)), ((), ())),
            preferred_element_type=jnp.float32,
        )
        product = product.reshape(seg_count, 2, 2, point_count)
        real_part = product[:, 0, 0] - product[:, 1, 1]
        imag_part = product[:, 1, 0] + product[:, 0, 1]
        return jnp.stack([real_part, imag_part], axis=0)

    return lax.map(per_bin, (bins_owned, jnp.moveaxis(received, 1, 0)))


def per_device(samples, bin_ids, delays):
    length = samples.shape[2]
    transform_rows = dft_table(bin_ids, length)
    spectra = jnp.einsum("sml,lk->skm", samples, transform_rows, preferred_element_type=jnp.float32)
    spectra = spectra.reshape(samples.shape[0], bin_ids.shape[0], 2, samples.shape[1]).astype(
        jnp.bfloat16
    )
    seg_count = spectra.shape[0]
    steered = steer_block(
        lax.all_gather(spectra, "mic", axis=3, tiled=True), delays, bin_ids, length
    )
    steered = steered / math.sqrt(delays.shape[1])
    powers = jnp.sum(steered * steered, axis=(1, 2))
    welch_sum = lax.psum_scatter(powers, "tm", scatter_dimension=0, tiled=True)
    return welch_sum / (seg_count * lax.axis_size("tm"))


def solution(mesh):
    placed = (P("tm", "mic", None), P(), P("mic", None))
    return jax.shard_map(
        per_device, mesh=mesh, in_specs=placed, out_specs=P("tm", "mic"), check_vma=False
    )
```

profile of v0, /device:TPU:1, one launch (start us, length us, event | category | flops | bytes accessed | tf_op | source)
XLA Modules:
  0.0 343.3 jit_solution(9585885661330164719)
XLA Ops:
  8.0 1.9 divide_convert_fusion.1
  10.4 6.1 %convolution_convert_fusion = bf16[32,8,128]{2,0,1:T(8,128)(2,1)S(1)} fusion(bf16[4096,32,1]{0,1,2:T(8,128)(2,1)S(1)} %reshape.233, bf16[8,128,4096]{2,1,0:T(8,128)(2,1)} %param.5), kind=kOutput, calls=%fused_computation.19 | convolution fusion | flops 268468224 | bytes 8716288 | tf_op jit(solution)/shard_map/sml,lk->skm/dot_general | solution.py:47
  18.5 110.3 %all-gather.2.cloned.1.call-done = bf16[8,16,2,4096]{3,0,2,1:T(8,128)(2,1)} async-done(((bf16[8,16,2,128]{3,0,2,1:T(8,128)(2,1)}), bf16[8,16,2,4096]{3,0,2,1:T(8,128)(2,1)}) %all-gather.2.cloned.1.call-update) | async-done | bytes 2097168 | tf_op jit(solution)/shard_map/all_gather | solution.py:53
  128.8 181.1 %while.12 = (s32[]{:T(128)}, f32[16,2,8,128]{3,2,1,0:T(8,128)S(1)}, bf16[16,8,2,4096]{3,1,2,0:T(8,128)(2,1)}, s32[16]{0:T(128)S(1)}, s32[128,4096]{1,0:T(8,128)S(1)}, /*index=5*/s32[]{:T(128)}) while((s32[]{:T(128)}, f32[16,2,8,128]{3,2,1,0:T(8,128)S(1)}, bf16[16,8,2,4096]{3,1,2,0:T(8,128)(2,1)}, s32[16]{0:T(128)S(1)}, ...), condition=%wide.region_2.3_spmd, body=%wide.region_1.2_spmd.sunk | while | flops 46141440 | bytes 10674777 | solution.py:41
  129.4 8.9 %cosine_convert_fusion.2 = (bf16[128,4096]{1,0:T(8,128)(2,1)S(1)}, bf16[128,4096]{1,0:T(8,128)(2,1)S(1)}) fusion(s32[128,4096]{1,0:T(8,128)S(1)} %get-tuple-element.146, s32[]{:T(128)} %bitcast.38), kind=kLoop, calls=%fused_computation.8.clone.1 | loop fusion | flops 8388608 | bytes 4194308 | tf_op jit(solution)/shard_map/convert
  138.5 1.6 fusion.27
  140.7 8.9 %cosine_convert_fusion.2 = (bf16[128,4096]{1,0:T(8,128)(2,1)S(1)}, bf16[128,4096]{1,0:T(8,128)(2,1)S(1)}) fusion(s32[128,4096]{1,0:T(8,128)S(1)} %get-tuple-element.146, s32[]{:T(128)} %bitcast.38), kind=kLoop, calls=%fused_computation.8.clone.1 | loop fusion | flops 8388608 | bytes 4194308 | tf_op jit(solution)/shard_map/convert
  149.8 1.6 fusion.27
  152.0 8.9 %cosine_convert_fusion.2 = (bf16[128,4096]{1,0:T(8,128)(2,1)S(1)}, bf16[128,4096]{1,0:T(8,128)(2,1)S(1)}) fusion(s32[128,4096]{1,0:T(8,128)S(1)} %get-tuple-element.146, s32[]{:T(128)} %bitcast.38), kind=kLoop, calls=%fused_computation.8.clone.1 | loop fusion | flops 8388608 | bytes 4194308 | tf_op jit(solution)/shard_map/convert
  163.3 8.9 %cosine_convert_fusion.2 = (bf16[128,4096]{1,0:T(8,128)(2,1)S(1)}, bf16[128,4096]{1,0:T(8,128)(2,1)S(1)}) fusion(s32[128,4096]{1,0:T(8,128)S(1)} %get-tuple-element.146, s32[]{:T(128)} %bitcast.38), kind=kLoop, calls=%fused_computation.8.clone.1 | loop fusion | flops 8388608 | bytes 4194308 | tf_op jit(solution)/shard_map/convert
  174.6 8.9 %cosine_convert_fusion.2 = (bf16[128,4096]{1,0:T(8,128)(2,1)S(1)}, bf16[128,4096]{1,0:T(8,128)(2,1)S(1)}) fusion(s32[128,4096]{1,0:T(8,128)S(1)} %get-tuple-element.146, s32[]{:T(128)} %bitcast.38), kind=kLoop, calls=%fused_computation.8.clone.1 | loop fusion | flops 8388608 | bytes 4194308 | tf_op jit(solution)/shard_map/convert
  185.9 8.9 %cosine_convert_fusion.2 = (bf16[128,4096]{1,0:T(8,128)(2,1)S(1)}, bf16[128,4096]{1,0:T(8,128)(2,1)S(1)}) fusion(s32[128,4096]{1,0:T(8,128)S(1)} %get-tuple-element.146, s32[]{:T(128)} %bitcast.38), kind=kLoop, calls=%fused_computation.8.clone.1 | loop fusion | flops 8388608 | bytes 4194308 | tf_op jit(solution)/shard_map/convert
  195.1 1.6 fusion.27
  197.3 8.9 %cosine_convert_fusion.2 = (bf16[128,4096]{1,0:T(8,128)(2,1)S(1)}, bf16[128,4096]{1,0:T(8,128)(2,1)S(1)}) fusion(s32[128,4096]{1,0:T(8,128)S(1)} %get-tuple-element.146, s32[]{:T(128)} %bitcast.38), kind=kLoop, calls=%fused_computation.8.clone.1 | loop fusion | flops 8388608 | bytes 4194308 | tf_op jit(solution)/shard_map/convert
  208.6 8.9 %cosine_convert_fusion.2 = (bf16[128,4096]{1,0:T(8,128)(2,1)S(1)}, bf16[128,4096]{1,0:T(8,128)(2,1)S(1)}) fusion(s32[128,4096]{1,0:T(8,128)S(1)} %get-tuple-element.146, s32[]{:T(128)} %bitcast.38), kind=kLoop, calls=%fused_computation.8.clone.1 | loop fusion | flops 8388608 | bytes 4194308 | tf_op jit(solution)/shard_map/convert
  219.9 8.9 %cosine_convert_fusion.2 = (bf16[128,4096]{1,0:T(8,128)(2,1)S(1)}, bf16[128,4096]{1,0:T(8,128)(2,1)S(1)}) fusion(s32[128,4096]{1,0:T(8,128)S(1)} %get-tuple-element.146, s32[]{:T(128)} %bitcast.38), kind=kLoop, calls=%fused_computation.8.clone.1 | loop fusion | flops 8388608 | bytes 4194308 | tf_op jit(solution)/shard_map/convert
  231.2 8.9 %cosine_convert_fusion.2 = (bf16[128,4096]{1,0:T(8,128)(2,1)S(1)}, bf16[128,4096]{1,0:T(8,128)(2,1)S(1)}) fusion(s32[128,4096]{1,0:T(8,128)S(1)} %get-tuple-element.146, s32[]{:T(128)} %bitcast.38), kind=kLoop, calls=%fused_computation.8.clone.1 | loop fusion | flops 8388608 | bytes 4194308 | tf_op jit(solution)/shard_map/convert
  242.5 8.9 %cosine_convert_fusion.2 = (bf16[128,4096]{1,0:T(8,128)(2,1)S(1)}, bf16[128,4096]{1,0:T(8,128)(2,1)S(1)}) fusion(s32[128,4096]{1,0:T(8,128)S(1)} %get-tuple-element.146, s32[]{:T(128)} %bitcast.38), kind=kLoop, calls=%fused_computation.8.clone.1 | loop fusion | flops 8388608 | bytes 4194308 | tf_op jit(solution)/shard_map/convert
  253.8 8.9 %cosine_convert_fusion.2 = (bf16[128,4096]{1,0:T(8,128)(2,1)S(1)}, bf16[128,4096]{1,0:T(8,128)(2,1)S(1)}) fusion(s32[128,4096]{1,0:T(8,128)S(1)} %get-tuple-element.146, s32[]{:T(128)} %bitcast.38), kind=kLoop, calls=%fused_computation.8.clone.1 | loop fusion | flops 8388608 | bytes 4194308 | tf_op jit(solution)/shard_map/convert
  265.2 8.9 %cosine_convert_fusion.2 = (bf16[128,4096]{1,0:T(8,128)(2,1)S(1)}, bf16[128,4096]{1,0:T(8,128)(2,1)S(1)}) fusion(s32[128,4096]{1,0:T(8,128)S(1)} %get-tuple-element.146, s32[]{:T(128)} %bitcast.38), kind=kLoop, calls=%fused_computation.8.clone.1 | loop fusion | flops 8388608 | bytes 4194308 | tf_op jit(solution)/shard_map/convert
  276.5 8.9 %cosine_convert_fusion.2 = (bf16[128,4096]{1,0:T(8,128)(2,1)S(1)}, bf16[128,4096]{1,0:T(8,128)(2,1)S(1)}) fusion(s32[128,4096]{1,0:T(8,128)S(1)} %get-tuple-element.146, s32[]{:T(128)} %bitcast.38), kind=kLoop, calls=%fused_computation.8.clone.1 | loop fusion | flops 8388608 | bytes 4194308 | tf_op jit(solution)/shard_map/convert
  287.8 8.9 %cosine_convert_fusion.2 = (bf16[128,4096]{1,0:T(8,128)(2,1)S(1)}, bf16[128,4096]{1,0:T(8,128)(2,1)S(1)}) fusion(s32[128,4096]{1,0:T(8,128)S(1)} %get-tuple-element.146, s32[]{:T(128)} %bitcast.38), kind=kLoop, calls=%fused_computation.8.clone.1 | loop fusion | flops 8388608 | bytes 4194308 | tf_op jit(solution)/shard_map/convert
  299.1 8.9 %cosine_convert_fusion.2 = (bf16[128,4096]{1,0:T(8,128)(2,1)S(1)}, bf16[128,4096]{1,0:T(8,128)(2,1)S(1)}) fusion(s32[128,4096]{1,0:T(8,128)S(1)} %get-tuple-element.146, s32[]{:T(128)} %bitcast.38), kind=kLoop, calls=%fused_computation.8.clone.1 | loop fusion | flops 8388608 | bytes 4194308 | tf_op jit(solution)/shard_map/convert
  309.9 26.0 %all-reduce = f32[16,128]{1,0:T(8,128)S(1)} all-reduce(f32[16,128]{1,0:T(8,128)S(1)} %multiply_reduce_fusion), channel_id=2, replica_groups=mesh['tm'=4,'mic'=32] {'tm'}, use_global_device_ids=true, to_apply=%region_4.5.clone | all-reduce | flops 2048 | bytes 16384
  (95 shorter events, 36.0 us)
Async XLA Ops:
  6.5 122.3 %all-gather.2.cloned.1.call-start = ((), (), s32[]{:S(2)}) async-start(), calls=%async_computation | async-start | bytes 2162688 | tf_op jit(solution)/shard_map/all_gather | solution.py:53
  10.3 6.8 %copy-start.2 = (u32[128]{0:T(128)S(1)}, u32[128]{0:T(128)}, u32[]{:S(2)}) copy-start(u32[128]{0:T(128)} %constant.85) | copy-start | bytes 1540
  10.3 118.5 %copy-start = (s32[128,4096]{1,0:T(8,128)S(1)}, s32[128,4096]{1,0:T(8,128)}, u32[]{:S(2)}) copy-start(s32[128,4096]{1,0:T(8,128)} %param.7) | copy-start | bytes 6291460
  10.3 118.4 %copy-start.1 = (s32[16]{0:T(128)S(1)}, s32[16]{0:T(128)}, u32[]{:S(2)}) copy-start(s32[16]{0:T(128)} %param.6) | copy-start | bytes 196
Sparse Core Ops, SparseCore 0:
  17.3 111.4 all-gather.1
where the time goes:
time: 344 us; the launch traced here: 343 us
  other arithmetic  150 us (44%)
  waiting for transfers between devices  110 us (32%)
  matrix products  31 us (9%)
  blocking collectives  26 us (8%)
  between operations  14.9 us (4%)
  local copies, waits for them, and re-layouts  10.6 us (3%)
    another operation x17, other arithmetic  145 us
    all_gather x1, waiting for transfers between devices, per_device(): lax.all_gather(spectra, 'mic', axis=3, tiled=True)  110 us
    unnamed x1, blocking collectives  26 us
    dot_general x16, matrix products, per_bin(): lax.dot_general(values.reshape(seg_count * 2, mic_count), steer_rows, (((...  24.9 us
    dynamic_slice x16, local copies, waits for them, and re-layouts, steer_block(): return lax.map(per_bin, (bins_owned, jnp.moveaxis(received, 1, 0)))  8.9 us
  transfers between devices with their start and end apart: 1, of which 1 were waited for; matrix products, arithmetic and copies ran while one was open for 0% of the time, Pallas kernels for 0%

commit v1 on v0

--- a/solution.py
+++ b/solution.py
@@ -50,7 +50,12 @@
     )
     seg_count = spectra.shape[0]
     steered = steer_block(
-        lax.all_gather(spectra, "mic", axis=3, tiled=True), delays, bin_ids, length
+        jnp.concatenate(
+            lax.all_to_all(jnp.stack([spectra] * lax.axis_size("mic")), "mic", 0, 0), axis=3
+        ),
+        delays,
+        bin_ids,
+        length,
     )
     steered = steered / math.sqrt(delays.shape[1])
     powers = jnp.sum(steered * steered, axis=(1, 2))

time: 344 us -> 254 us (0.74)
  waiting for transfers between devices: 110 us -> 27.3 us
  blocking collectives: 26 us -> 9.07 us
  between operations: 14.9 us -> 1.42 us
  local copies, waits for them, and re-layouts: 10.6 us -> 23.4 us
  starting transfers between devices: 0.01 us -> 9.34 us
    all_gather x1 -> x0, waiting for transfers between devices: 110 us -> none  [per_device(): lax.all_gather(spectra, 'mic', axis=3, tiled=True)]
    all_to_all x0 -> x1, waiting for transfers between devices: none -> 27.3 us  [per_device(): lax.all_to_all(jnp.stack([spectra] * lax.axis_size('mic')), 'mic', 0, 0)]
    unnamed x1, blocking collectives: 26 us -> 9.07 us
    all_to_all x0 -> x1, starting transfers between devices: none -> 9.34 us  [per_device(): lax.all_to_all(jnp.stack([spectra] * lax.axis_size('mic')), 'mic', 0, 0)]
    reshape x0 -> x2, local copies, waits for them, and re-layouts: none -> 6.85 us  [per_device(): jnp.concatenate(lax.all_to_all(jnp.stack([spectra] * lax.axis_size('mic')...]
    while x0 -> x1, local copies, waits for them, and re-layouts: none -> 4.23 us  [steer_block(): return lax.map(per_bin, (bins_owned, jnp.moveaxis(received, 1, 0)))]
where the time goes in v1:
time: 254 us; the launch traced here: 253 us
  other arithmetic  151 us (59%)
  matrix products  30.9 us (12%)
  waiting for transfers between devices  27.3 us (11%)
  local copies, waits for them, and re-layouts  23.4 us (9%)
  starting transfers between devices  9.34 us (4%)
  blocking collectives  9.07 us (4%)
    another operation x17, other arithmetic  146 us
    all_to_all x1, waiting for transfers between devices, per_device(): lax.all_to_all(jnp.stack([spectra] * lax.axis_size('mic')), 'mic', 0, 0)  27.3 us
    dot_general x16, matrix products, per_bin(): lax.dot_general(values.reshape(seg_count * 2, mic_count), steer_rows, (((...  24.9 us
    dynamic_slice x16, local copies, waits for them, and re-layouts, steer_block(): return lax.map(per_bin, (bins_owned, jnp.moveaxis(received, 1, 0)))  9.5 us
    all_to_all x1, starting transfers between devices, per_device(): lax.all_to_all(jnp.stack([spectra] * lax.axis_size('mic')), 'mic', 0, 0)  9.34 us
    unnamed x1, blocking collectives  9.07 us
    reshape x2, local copies, waits for them, and re-layouts, per_device(): jnp.concatenate(lax.all_to_all(jnp.stack([spectra] * lax.axis_size('mic')...  6.85 us
    dot_general x1, matrix products, per_device(): jnp.einsum('sml,lk->skm', samples, transform_rows, preferred_element_type...  5.95 us
  transfers between devices with their start and end apart: 1, of which 1 were waited for; matrix products, arithmetic and copies ran while one was open for 0% of the time, Pallas kernels for 0%

profile of v1, /device:TPU:1, one launch (start us, length us, event | category | flops | bytes accessed | tf_op | source)
XLA Modules:
  0.0 253.1 jit_solution(15147883942504400595)
XLA Ops:
  3.8 5.9 %convolution_convert_fusion = bf16[32,8,128]{2,0,1:T(8,128)(2,1)S(1)} fusion(bf16[4096,32,1]{0,1,2:T(8,128)(2,1)S(1)} %reshape.244, bf16[8,128,4096]{2,1,0:T(8,128)(2,1)} %param.5), kind=kOutput, calls=%fused_computation.19 | convolution fusion | flops 268468224 | bytes 8716288 | tf_op jit(solution)/shard_map/sml,lk->skm/dot_general | solution.py:47
  11.6 9.3 %all-to-all-start = ((bf16[32,8,16,2,128]{4,1,3,2,0:T(8,128)(2,1)}), bf16[32,8,16,2,128]{4,1,3,2,0:T(8,128)(2,1)S(1)}, u32[]{:S(2)}, u32[]{:S(2)}) async-start(bf16[32,8,16,2,128]{4,1,3,2,0:T(8,128)(2,1)} %stack.11), calls=%async_computation | async-start | bytes 4194304 | tf_op jit(solution)/shard_map/all_to_all | solution.py:54
  22.2 27.3 %all-to-all-done = bf16[32,8,16,2,128]{4,1,3,2,0:T(8,128)(2,1)S(1)} async-done(((bf16[32,8,16,2,128]{4,1,3,2,0:T(8,128)(2,1)}), bf16[32,8,16,2,128]{4,1,3,2,0:T(8,128)(2,1)S(1)}, u32[]{:S(2)}, u32[]{:S(2)}) %all-to-all-start) | async-done | bytes 2097184 | tf_op jit(solution)/shard_map/all_to_all | solution.py:54
  49.5 2.7 %copy.14 = bf16[8,16,2,32,128]{4,3,1,2,0:T(8,128)(2,1)} copy(bf16[8,16,2,32,128]{4,0,2,1,3:T(8,128)(2,1)S(1)} %bitcast.46) | data formatting | bytes 4194304 | tf_op jit(solution)/shard_map/reshape | solution.py:53
  52.2 4.2 %reshape.241 = bf16[8,16,2,4096]{3,1,2,0:T(8,128)(2,1)} reshape(bf16[8,16,2,32,128]{4,3,1,2,0:T(8,128)(2,1)} %copy.14) | data formatting | bytes 4194304 | tf_op jit(solution)/shard_map/reshape | solution.py:53
  56.3 4.2 %copy.15 = bf16[16,8,2,4096]{3,1,2,0:T(8,128)(2,1)} copy(bf16[16,8,2,4096]{3,0,2,1:T(8,128)(2,1)} %bitcast.47) | data formatting | bytes 4194304 | tf_op jit(solution)/shard_map/while | solution.py:41
  60.6 182.8 %while.12 = (s32[]{:T(128)}, f32[16,2,8,128]{3,2,1,0:T(8,128)S(1)}, bf16[16,8,2,4096]{3,1,2,0:T(8,128)(2,1)}, s32[16]{0:T(128)S(1)}, s32[128,4096]{1,0:T(8,128)S(1)}, /*index=5*/s32[]{:T(128)}) while((s32[]{:T(128)}, f32[16,2,8,128]{3,2,1,0:T(8,128)S(1)}, bf16[16,8,2,4096]{3,1,2,0:T(8,128)(2,1)}, s32[16]{0:T(128)S(1)}, ...), condition=%wide.region_2.3_spmd, body=%wide.region_1.2_spmd.sunk | while | flops 46141440 | bytes 10674777 | solution.py:41
  61.1 9.0 %cosine_convert_fusion.2 = (bf16[128,4096]{1,0:T(8,128)(2,1)S(1)}, bf16[128,4096]{1,0:T(8,128)(2,1)S(1)}) fusion(s32[128,4096]{1,0:T(8,128)S(1)} %get-tuple-element.161, s32[]{:T(128)} %bitcast.43), kind=kLoop, calls=%fused_computation.8.clone.1 | loop fusion | flops 8388608 | bytes 4194308 | tf_op jit(solution)/shard_map/convert
  72.6 9.0 %cosine_convert_fusion.2 = (bf16[128,4096]{1,0:T(8,128)(2,1)S(1)}, bf16[128,4096]{1,0:T(8,128)(2,1)S(1)}) fusion(s32[128,4096]{1,0:T(8,128)S(1)} %get-tuple-element.161, s32[]{:T(128)} %bitcast.43), kind=kLoop, calls=%fused_computation.8.clone.1 | loop fusion | flops 8388608 | bytes 4194308 | tf_op jit(solution)/shard_map/convert
  84.0 9.0 %cosine_convert_fusion.2 = (bf16[128,4096]{1,0:T(8,128)(2,1)S(1)}, bf16[128,4096]{1,0:T(8,128)(2,1)S(1)}) fusion(s32[128,4096]{1,0:T(8,128)S(1)} %get-tuple-element.161, s32[]{:T(128)} %bitcast.43), kind=kLoop, calls=%fused_computation.8.clone.1 | loop fusion | flops 8388608 | bytes 4194308 | tf_op jit(solution)/shard_map/convert
  95.4 9.0 %cosine_convert_fusion.2 = (bf16[128,4096]{1,0:T(8,128)(2,1)S(1)}, bf16[128,4096]{1,0:T(8,128)(2,1)S(1)}) fusion(s32[128,4096]{1,0:T(8,128)S(1)} %get-tuple-element.161, s32[]{:T(128)} %bitcast.43), kind=kLoop, calls=%fused_computation.8.clone.1 | loop fusion | flops 8388608 | bytes 4194308 | tf_op jit(solution)/shard_map/convert
  106.8 9.0 %cosine_convert_fusion.2 = (bf16[128,4096]{1,0:T(8,128)(2,1)S(1)}, bf16[128,4096]{1,0:T(8,128)(2,1)S(1)}) fusion(s32[128,4096]{1,0:T(8,128)S(1)} %get-tuple-element.161, s32[]{:T(128)} %bitcast.43), kind=kLoop, calls=%fused_computation.8.clone.1 | loop fusion | flops 8388608 | bytes 4194308 | tf_op jit(solution)/shard_map/convert
  118.3 9.0 %cosine_convert_fusion.2 = (bf16[128,4096]{1,0:T(8,128)(2,1)S(1)}, bf16[128,4096]{1,0:T(8,128)(2,1)S(1)}) fusion(s32[128,4096]{1,0:T(8,128)S(1)} %get-tuple-element.161, s32[]{:T(128)} %bitcast.43), kind=kLoop, calls=%fused_computation.8.clone.1 | loop fusion | flops 8388608 | bytes 4194308 | tf_op jit(solution)/shard_map/convert
  129.7 9.0 %cosine_convert_fusion.2 = (bf16[128,4096]{1,0:T(8,128)(2,1)S(1)}, bf16[128,4096]{1,0:T(8,128)(2,1)S(1)}) fusion(s32[128,4096]{1,0:T(8,128)S(1)} %get-tuple-element.161, s32[]{:T(128)} %bitcast.43), kind=kLoop, calls=%fused_computation.8.clone.1 | loop fusion | flops 8388608 | bytes 4194308 | tf_op jit(solution)/shard_map/convert
  141.1 9.0 %cosine_convert_fusion.2 = (bf16[128,4096]{1,0:T(8,128)(2,1)S(1)}, bf16[128,4096]{1,0:T(8,128)(2,1)S(1)}) fusion(s32[128,4096]{1,0:T(8,128)S(1)} %get-tuple-element.161, s32[]{:T(128)} %bitcast.43), kind=kLoop, calls=%fused_computation.8.clone.1 | loop fusion | flops 8388608 | bytes 4194308 | tf_op jit(solution)/shard_map/convert
  152.5 9.0 %cosine_convert_fusion.2 = (bf16[128,4096]{1,0:T(8,128)(2,1)S(1)}, bf16[128,4096]{1,0:T(8,128)(2,1)S(1)}) fusion(s32[128,4096]{1,0:T(8,128)S(1)} %get-tuple-element.161, s32[]{:T(128)} %bitcast.43), kind=kLoop, calls=%fused_computation.8.clone.1 | loop fusion | flops 8388608 | bytes 4194308 | tf_op jit(solution)/shard_map/convert
  164.0 9.0 %cosine_convert_fusion.2 = (bf16[128,4096]{1,0:T(8,128)(2,1)S(1)}, bf16[128,4096]{1,0:T(8,128)(2,1)S(1)}) fusion(s32[128,4096]{1,0:T(8,128)S(1)} %get-tuple-element.161, s32[]{:T(128)} %bitcast.43), kind=kLoop, calls=%fused_computation.8.clone.1 | loop fusion | flops 8388608 | bytes 4194308 | tf_op jit(solution)/shard_map/convert
  175.4 9.0 %cosine_convert_fusion.2 = (bf16[128,4096]{1,0:T(8,128)(2,1)S(1)}, bf16[128,4096]{1,0:T(8,128)(2,1)S(1)}) fusion(s32[128,4096]{1,0:T(8,128)S(1)} %get-tuple-element.161, s32[]{:T(128)} %bitcast.43), kind=kLoop, calls=%fused_computation.8.clone.1 | loop fusion | flops 8388608 | bytes 4194308 | tf_op jit(solution)/shard_map/convert
  186.8 9.0 %cosine_convert_fusion.2 = (bf16[128,4096]{1,0:T(8,128)(2,1)S(1)}, bf16[128,4096]{1,0:T(8,128)(2,1)S(1)}) fusion(s32[128,4096]{1,0:T(8,128)S(1)} %get-tuple-element.161, s32[]{:T(128)} %bitcast.43), kind=kLoop, calls=%fused_computation.8.clone.1 | loop fusion | flops 8388608 | bytes 4194308 | tf_op jit(solution)/shard_map/convert
  198.3 9.0 %cosine_convert_fusion.2 = (bf16[128,4096]{1,0:T(8,128)(2,1)S(1)}, bf16[128,4096]{1,0:T(8,128)(2,1)S(1)}) fusion(s32[128,4096]{1,0:T(8,128)S(1)} %get-tuple-element.161, s32[]{:T(128)} %bitcast.43), kind=kLoop, calls=%fused_computation.8.clone.1 | loop fusion | flops 8388608 | bytes 4194308 | tf_op jit(solution)/shard_map/convert
  209.7 9.0 %cosine_convert_fusion.2 = (bf16[128,4096]{1,0:T(8,128)(2,1)S(1)}, bf16[128,4096]{1,0:T(8,128)(2,1)S(1)}) fusion(s32[128,4096]{1,0:T(8,128)S(1)} %get-tuple-element.161, s32[]{:T(128)} %bitcast.43), kind=kLoop, calls=%fused_computation.8.clone.1 | loop fusion | flops 8388608 | bytes 4194308 | tf_op jit(solution)/shard_map/convert
  221.1 9.0 %cosine_convert_fusion.2 = (bf16[128,4096]{1,0:T(8,128)(2,1)S(1)}, bf16[128,4096]{1,0:T(8,128)(2,1)S(1)}) fusion(s32[128,4096]{1,0:T(8,128)S(1)} %get-tuple-element.161, s32[]{:T(128)} %bitcast.43), kind=kLoop, calls=%fused_computation.8.clone.1 | loop fusion | flops 8388608 | bytes 4194308 | tf_op jit(solution)/shard_map/convert
  232.5 9.0 %cosine_convert_fusion.2 = (bf16[128,4096]{1,0:T(8,128)(2,1)S(1)}, bf16[128,4096]{1,0:T(8,128)(2,1)S(1)}) fusion(s32[128,4096]{1,0:T(8,128)S(1)} %get-tuple-element.161, s32[]{:T(128)} %bitcast.43), kind=kLoop, calls=%fused_computation.8.clone.1 | loop fusion | flops 8388608 | bytes 4194308 | tf_op jit(solution)/shard_map/convert
  243.4 9.1 %all-reduce = f32[16,128]{1,0:T(8,128)S(1)} all-reduce(f32[16,128]{1,0:T(8,128)S(1)} %multiply_reduce_fusion), channel_id=2, replica_groups=mesh['tm'=4,'mic'=32] {'tm'}, use_global_device_ids=true, to_apply=%region_4.5.clone | all-reduce | flops 2048 | bytes 16384
  (98 shorter events, 44.3 us)
Async XLA Ops:
  11.6 9.4 %copy-start.2 = (u32[128]{0:T(128)S(1)}, u32[128]{0:T(128)}, u32[]{:S(2)}) copy-start(u32[128]{0:T(128)} %constant.85) | copy-start | bytes 1540
  11.6 37.9 %all-to-all-start = ((bf16[32,8,16,2,128]{4,1,3,2,0:T(8,128)(2,1)}), bf16[32,8,16,2,128]{4,1,3,2,0:T(8,128)(2,1)S(1)}, u32[]{:S(2)}, u32[]{:S(2)}) async-start(bf16[32,8,16,2,128]{4,1,3,2,0:T(8,128)(2,1)} %stack.11), calls=%async_computation | async-start | bytes 4194304 | tf_op jit(solution)/shard_map/all_to_all | solution.py:54
  56.3 4.2 %copy-start = (s32[128,4096]{1,0:T(8,128)S(1)}, s32[128,4096]{1,0:T(8,128)}, u32[]{:S(2)}) copy-start(s32[128,4096]{1,0:T(8,128)} %param.7) | copy-start | bytes 6291460
  56.3 4.2 %copy-start.1 = (s32[16]{0:T(128)S(1)}, s32[16]{0:T(128)}, u32[]{:S(2)}) copy-start(s32[16]{0:T(128)} %param.6) | copy-start | bytes 196
